TPU v7x, 32 devices: a whole 2x2x4 slice. The times are simulated.
32 devices in a mesh: gx: 4 (over z), gy: 8 (over y, x, core).
Axes of the slice: x: 2, y: 2, z: 4, core: 2. Of those that a mesh axis runs over, the one named last changes fastest.
Arguments:
- data: bfloat16 [128, 512, 1024], P(None, 'gx', 'gy')
- inv_scale: float32 [128], replicated, may hold values from 0.1 to 1
- start: float32 [128, 32], replicated, may hold values from -6 to 6
- rank: int32 [1], replicated, may hold values from 24 to 32
Outputs:
- core: bfloat16 [32, 512, 1024], P(None, 'gx', 'gy')
- factor: float32 [128, 32], replicated
Inputs may be any that keep to these rules, and one draw needn't show every extreme that they name: rank[0] is the number of leading columns of the factor that are kept.
All inputs are finite; a program needn't handle non-finite values.
Results may differ from a plain program's by a relative error of at most 0.0044.
Values sent between devices are 32-bit elements; how exact they have to be, the bound alone decides.
A program may use at most 64 MiB of HBM per device.

v0:
```python
import jax
import jax.numpy as jnp
from jax import lax
from jax.sharding import PartitionSpec as P

ITERS = 4


def body(data, inv_scale, start, rank):
    variables = data.shape[0]
    columns = start.shape[1]
    flat = data.reshape(variables, -1)
    local_gram = lax.dot_general(
        flat, flat, (((1,), (1,)), ((), ())), preferred_element_type=jnp.float32
    )
    gram = lax.psum(local_gram, ("gx", "gy"))
    weighted = inv_scale[:, None] * gram * inv_scale[None, :]
    basis = start
    for turn in range(ITERS):
        image = jnp.dot(weighted, basis, precision=lax.Precision.HIGHEST)
        inner = jnp.dot(image.T, image, precision=lax.Precision.HIGHEST)
        lower = jnp.linalg.cholesky(inner)
        basis = lax.linalg.triangular_solve(
            lower, image, left_side=False, lower=True, transpose_a=True
        )
    keep = (jnp.arange(columns, dtype=jnp.int32) < rank[0]).astype(jnp.float32)
    factor = basis * keep[None, :]
    scaled_factor = (inv_scale[:, None] * factor).astype(jnp.bfloat16)
    product = lax.dot_general(
        scaled_factor, flat, (((0,), (0,)), ((), ())), preferred_element_type=jnp.float32
    )
    core = product.astype(jnp.bfloat16).reshape(columns, data.shape[1], data.shape[2])
    return (core, factor)


def solution(mesh):
    in_specs = (P(None, "gx", "gy"), P(), P(), P())
    out_specs = (P(None, "gx", "gy"), P())
    return jax.shard_map(body, mesh=mesh, in_specs=in_specs, out_specs=out_specs, check_vma=False)
```

profile of v0, /device:TPU:1, one launch (start us, length us, event | category | flops | bytes accessed | tf_op | source)
XLA Modules:
  0.0 185.7 jit_solution(14243155040835074727)
XLA Ops:
  7.2 8.8 %fusion.7 = f32[128,128]{1,0:T(8,128)} fusion(bf16[128,128,128]{2,1,0:T(8,128)(2,1)} %param.7), kind=kOutput, calls=%fused_computation.6 | convolution fusion | flops 536870912 | bytes 4259840 | tf_op jit(solution)/shard_map/dot_general | solution.py:13
  16.7 122.8 %all-reduce.2.cloned.1.call-done = f32[128,128]{1,0:T(8,128)} async-done(((f32[128,128]{1,0:T(8,128)}), f32[128,128]{1,0:T(8,128)}) %all-reduce.2.cloned.1.call-update) | async-done | bytes 65552 | tf_op jit(solution)/shard_map/psum | solution.py:16
  139.5 1.1 fusion.14
  140.6 0.2 fusion.42
  140.9 2.9 %cholesky.74 = f32[32,32]{1,0:T(8,128)S(1)} custom-call(f32[32,32]{1,0:T(8,128)S(1)} %fusion.34), custom_call_target="Cholesky" | custom-call | tf_op jit(solution)/shard_map/jit(cholesky)/cholesky | solution.py:22
  143.9 0.6 compare_reduce_fusion.3
  144.5 0.7 fusion.23
  145.2 2.4 %custom-call.8 = f32[1,32,32]{1,2,0:T(8,128)S(1)} custom-call(f32[1,32,32]{2,1,0:T(8,128)S(1)} %fusion.23), custom_call_target="InvertDiagBlocksLowerTriangular" | custom-call | tf_op jit(solution)/shard_map/triangular_solve/custom-call.0 | solution.py:23
  147.6 0.2 convolution_bitcast_fusion.3
  147.8 1.1 fusion.13
  148.9 0.2 fusion.43
  149.2 2.9 %cholesky.85 = f32[32,32]{1,0:T(8,128)S(1)} custom-call(f32[32,32]{1,0:T(8,128)S(1)} %fusion.32), custom_call_target="Cholesky" | custom-call | tf_op jit(solution)/shard_map/jit(cholesky)/cholesky | solution.py:22
  152.2 0.6 compare_reduce_fusion.2
  152.8 0.7 fusion.24
  153.5 2.4 %custom-call.9 = f32[1,32,32]{1,2,0:T(8,128)S(1)} custom-call(f32[1,32,32]{2,1,0:T(8,128)S(1)} %fusion.24), custom_call_target="InvertDiagBlocksLowerTriangular" | custom-call | tf_op jit(solution)/shard_map/triangular_solve/custom-call.0 | solution.py:23
  155.9 0.2 convolution_bitcast_fusion.2
  156.1 1.1 fusion.12
  157.3 0.2 fusion.44
  157.5 2.9 %cholesky.96 = f32[32,32]{1,0:T(8,128)S(1)} custom-call(f32[32,32]{1,0:T(8,128)S(1)} %fusion.30), custom_call_target="Cholesky" | custom-call | tf_op jit(solution)/shard_map/jit(cholesky)/cholesky | solution.py:22
  160.5 0.6 compare_reduce_fusion.1
  161.1 0.7 fusion.25
  161.8 2.4 %custom-call.10 = f32[1,32,32]{1,2,0:T(8,128)S(1)} custom-call(f32[1,32,32]{2,1,0:T(8,128)S(1)} %fusion.25), custom_call_target="InvertDiagBlocksLowerTriangular" | custom-call | tf_op jit(solution)/shard_map/triangular_solve/custom-call.0 | solution.py:23
  164.2 0.2 convolution_bitcast_fusion.1
  164.5 1.1 fusion.11
  165.6 0.2 fusion.45
  165.8 2.9 %cholesky.107 = f32[32,32]{1,0:T(8,128)S(1)} custom-call(f32[32,32]{1,0:T(8,128)S(1)} %fusion.28), custom_call_target="Cholesky" | custom-call | tf_op jit(solution)/shard_map/jit(cholesky)/cholesky | solution.py:22
  168.8 0.6 compare_reduce_fusion
  169.4 0.7 fusion.26
  170.1 2.4 %custom-call.11 = f32[1,32,32]{1,2,0:T(8,128)S(1)} custom-call(f32[1,32,32]{2,1,0:T(8,128)S(1)} %fusion.26), custom_call_target="InvertDiagBlocksLowerTriangular" | custom-call | tf_op jit(solution)/shard_map/triangular_solve/custom-call.0 | solution.py:23
  172.5 0.2 fusion.10
  172.8 4.8 %fusion.4 = bf16[4,8,128,128]{3,1,2,0:T(8,128)(2,1)S(1)} fusion(bf16[16,8,128,128]{3,2,1,0:T(8,128)(2,1)} %bitcast.75, f32[128,32]{0,1:T(8,128)S(1)} %fusion.10, f32[128]{0:T(128)S(1)} %copy-done.1), kind=kOutput, calls=%fused_computation.5 | convolution fusion | flops 134750208 | bytes 5259776 | tf_op jit(solution)/shard_map/dot_general | solution.py:29
  177.6 1.2 copy.13
  (21 shorter events, 0.5 us)
Async XLA Ops:
  7.2 132.4 %copy-start = (f32[128,32]{0,1:T(8,128)S(1)}, f32[128,32]{0,1:T(8,128)}, u32[]{:S(2)}) copy-start(f32[128,32]{0,1:T(8,128)} %param.9) | copy-start | bytes 49156
  7.2 132.3 %copy-start.1 = (f32[128]{0:T(128)S(1)}, f32[128]{0:T(128)}, u32[]{:S(2)}) copy-start(f32[128]{0:T(128)} %param.8) | copy-start | bytes 1540
  7.2 132.3 %all-reduce.2.cloned.1.call-start = ((), (), s32[]{:S(2)}) async-start(), calls=%async_computation | async-start | bytes 131072 | tf_op jit(solution)/shard_map/psum | solution.py:16
  172.8 6.0 %copy-start.2 = (f32[128,32]{0,1:T(8,128)}, f32[128,32]{0,1:T(8,128)S(1)}, u32[]{:S(2)}) copy-start(f32[128,32]{0,1:T(8,128)S(1)} %fusion.10) | copy-start | bytes 49156
Sparse Core Ops, SparseCore 0:
  16.1 123.3 all-reduce.1
where the time goes:
time: 186 us
  waiting for transfers between devices  123 us (66%)
  other arithmetic  26.8 us (14%)
  matrix products  19.6 us (11%)
  between operations  14.9 us (8%)
    psum x1, waiting for transfers between devices, body(): gram = lax.psum(local_gram, ('gx', 'gy'))  123 us
    another operation x12, other arithmetic, body(): lower = jnp.linalg.cholesky(inner)  14.4 us
    another operation x8, other arithmetic, body(): lax.linalg.triangular_solve(lower, image, left_side=False, lower=True, tr...  12.3 us
    dot_general x1, matrix products, body(): lax.dot_general(flat, flat, (((1,), (1,)), ((), ())), preferred_element_t...  8.76 us
    dot_general x1, matrix products, body(): lax.dot_general(scaled_factor, flat, (((0,), (0,)), ((), ())), preferred_...  4.81 us
    dot_general x4, matrix products, body(): image = jnp.dot(weighted, basis, precision=lax.Precision.HIGHEST)  4.42 us
  transfers between devices with their start and end apart: 1, of which 1 were waited for; matrix products, arithmetic and copies ran while one was open for 0% of the time, Pallas kernels for 0%

commit v1 on v0

--- a/solution.py
+++ b/solution.py
@@ -13,7 +13,7 @@
     local_gram = lax.dot_general(
         flat, flat, (((1,), (1,)), ((), ())), preferred_element_type=jnp.float32
     )
-    gram = lax.psum(local_gram, ("gx", "gy"))
+    gram = jnp.sum(lax.all_gather(local_gram, ("gx", "gy")), axis=0)
     weighted = inv_scale[:, None] * gram * inv_scale[None, :]
     basis = start
     for turn in range(ITERS):

time: 186 us -> 120 us (0.65)
  waiting for transfers between devices: 123 us -> 58.2 us
  matrix products: 19.6 us -> 16.2 us
    psum x1 -> x0, waiting for transfers between devices: 123 us -> none  [body(): gram = lax.psum(local_gram, ('gx', 'gy'))]
    all_gather x0 -> x1, waiting for transfers between devices: none -> 58.1 us  [body(): gram = jnp.sum(lax.all_gather(local_gram, ('gx', 'gy')), axis=0)]
    dot_general x4, matrix products: 4.42 us -> 1.06 us  [body(): image = jnp.dot(weighted, basis, precision=lax.Precision.HIGHEST)]
where the time goes in v1:
time: 120 us; the launch traced here: 119 us
  waiting for transfers between devices  58.2 us (48%)
  other arithmetic  28.5 us (24%)
  matrix products  16.2 us (14%)
  between operations  14.9 us (12%)
  local copies, waits for them, and re-layouts  1.51 us (1%)
    all_gather x1, waiting for transfers between devices, body(): gram = jnp.sum(lax.all_gather(local_gram, ('gx', 'gy')), axis=0)  58.1 us
    another operation x12, other arithmetic, body(): lower = jnp.linalg.cholesky(inner)  14.4 us
    another operation x8, other arithmetic, body(): lax.linalg.triangular_solve(lower, image, left_side=False, lower=True, tr...  12.3 us
    dot_general x1, matrix products, body(): lax.dot_general(flat, flat, (((1,), (1,)), ((), ())), preferred_element_t...  8.76 us
    dot_general x1, matrix products, body(): lax.dot_general(scaled_factor, flat, (((0,), (0,)), ((), ())), preferred_...  4.81 us
  transfers between devices with their start and end apart: 1, of which 1 were waited for; matrix products, arithmetic and copies ran while one was open for 0% of the time, Pallas kernels for 0%

profile of v1, /device:TPU:1, one launch (start us, length us, event | category | flops | bytes accessed | tf_op | source)
XLA Modules:
  0.0 119.3 jit_solution(12483709167873759517)
XLA Ops:
  7.2 8.8 %fusion.7 = f32[128,128]{1,0:T(8,128)} fusion(bf16[128,128,128]{2,1,0:T(8,128)(2,1)} %param.7), kind=kOutput, calls=%fused_computation.6 | convolution fusion | flops 536870912 | bytes 4259840 | tf_op jit(solution)/shard_map/dot_general | solution.py:13
  16.7 58.1 %all-gather.3.cloned.1.call-done = f32[4096,128]{1,0:T(8,128)} async-done(((f32[128,128]{1,0:T(8,128)}), f32[4096,128]{1,0:T(8,128)}) %all-gather.3.cloned.1.call-update) | async-done | bytes 2097168 | tf_op jit(solution)/shard_map/all_gather | solution.py:16
  74.8 1.7 %reduce_sum.9 = f32[128,128]{1,0:T(8,128)S(1)} reduce(f32[32,128,128]{2,1,0:T(8,128)} %bitcast.77, f32[]{:T(128)} %constant.30.clone.1), dimensions={0}, to_apply=%region_0.0 | reduce | flops 507904 | bytes 2162692 | tf_op jit(solution)/shard_map/reduce_sum | solution.py:16
  76.5 0.3 fusion.14
  76.8 0.2 fusion.42
  77.1 2.9 %cholesky.74 = f32[32,32]{1,0:T(8,128)S(1)} custom-call(f32[32,32]{1,0:T(8,128)S(1)} %fusion.34), custom_call_target="Cholesky" | custom-call | tf_op jit(solution)/shard_map/jit(cholesky)/cholesky | solution.py:22
  80.0 0.6 compare_reduce_fusion.3
  80.7 0.7 fusion.23
  81.3 2.4 %custom-call.8 = f32[1,32,32]{1,2,0:T(8,128)S(1)} custom-call(f32[1,32,32]{2,1,0:T(8,128)S(1)} %fusion.23), custom_call_target="InvertDiagBlocksLowerTriangular" | custom-call | tf_op jit(solution)/shard_map/triangular_solve/custom-call.0 | solution.py:23
  83.8 0.2 convolution_bitcast_fusion.3
  84.0 0.3 fusion.13
  84.3 0.2 fusion.43
  84.6 2.9 %cholesky.85 = f32[32,32]{1,0:T(8,128)S(1)} custom-call(f32[32,32]{1,0:T(8,128)S(1)} %fusion.32), custom_call_target="Cholesky" | custom-call | tf_op jit(solution)/shard_map/jit(cholesky)/cholesky | solution.py:22
  87.5 0.6 compare_reduce_fusion.2
  88.2 0.7 fusion.24
  88.8 2.4 %custom-call.9 = f32[1,32,32]{1,2,0:T(8,128)S(1)} custom-call(f32[1,32,32]{2,1,0:T(8,128)S(1)} %fusion.24), custom_call_target="InvertDiagBlocksLowerTriangular" | custom-call | tf_op jit(solution)/shard_map/triangular_solve/custom-call.0 | solution.py:23
  91.3 0.2 convolution_bitcast_fusion.2
  91.5 0.3 fusion.12
  91.8 0.2 fusion.44
  92.0 2.9 %cholesky.96 = f32[32,32]{1,0:T(8,128)S(1)} custom-call(f32[32,32]{1,0:T(8,128)S(1)} %fusion.30), custom_call_target="Cholesky" | custom-call | tf_op jit(solution)/shard_map/jit(cholesky)/cholesky | solution.py:22
  95.0 0.6 compare_reduce_fusion.1
  95.6 0.7 fusion.25
  96.3 2.4 %custom-call.10 = f32[1,32,32]{1,2,0:T(8,128)S(1)} custom-call(f32[1,32,32]{2,1,0:T(8,128)S(1)} %fusion.25), custom_call_target="InvertDiagBlocksLowerTriangular" | custom-call | tf_op jit(solution)/shard_map/triangular_solve/custom-call.0 | solution.py:23
  98.7 0.2 convolution_bitcast_fusion.1
  99.0 0.3 fusion.11
  99.5 2.9 %cholesky.107 = f32[32,32]{1,0:T(8,128)S(1)} custom-call(f32[32,32]{1,0:T(8,128)S(1)} %fusion.28), custom_call_target="Cholesky" | custom-call | tf_op jit(solution)/shard_map/jit(cholesky)/cholesky | solution.py:22
  102.5 0.6 compare_reduce_fusion
  103.1 0.7 fusion.26
  103.8 2.4 %custom-call.11 = f32[1,32,32]{1,2,0:T(8,128)S(1)} custom-call(f32[1,32,32]{2,1,0:T(8,128)S(1)} %fusion.26), custom_call_target="InvertDiagBlocksLowerTriangular" | custom-call | tf_op jit(solution)/shard_map/triangular_solve/custom-call.0 | solution.py:23
  106.2 0.2 fusion.10
  106.5 4.8 %fusion.4 = bf16[4,8,128,128]{3,1,2,0:T(8,128)(2,1)S(1)} fusion(bf16[16,8,128,128]{3,2,1,0:T(8,128)(2,1)} %bitcast.76, f32[128,32]{0,1:T(8,128)S(1)} %fusion.10, f32[128]{0:T(128)S(1)} %copy-done.1), kind=kOutput, calls=%fused_computation.5 | convolution fusion | flops 134750208 | bytes 5259776 | tf_op jit(solution)/shard_map/dot_general | solution.py:29
  111.3 1.2 %copy.13 = bf16[4,8,128,128]{3,2,1,0:T(8,128)(2,1)} copy(bf16[4,8,128,128]{3,1,2,0:T(8,128)(2,1)S(1)} %fusion.4) | data formatting | bytes 2097152
  (22 shorter events, 0.7 us)
Async XLA Ops:
  7.2 69.4 %copy-start = (f32[128,32]{0,1:T(8,128)S(1)}, f32[128,32]{0,1:T(8,128)}, u32[]{:S(2)}) copy-start(f32[128,32]{0,1:T(8,128)} %param.9) | copy-start | bytes 49156
  7.2 69.4 %copy-start.1 = (f32[128]{0:T(128)S(1)}, f32[128]{0:T(128)}, u32[]{:S(2)}) copy-start(f32[128]{0:T(128)} %param.8) | copy-start | bytes 1540
  7.2 67.6 %all-gather.3.cloned.1.call-start = ((), (), s32[]{:S(2)}) async-start(), calls=%async_computation | async-start | bytes 2162688 | tf_op jit(solution)/shard_map/all_gather | solution.py:16
  106.4 6.0 %copy-start.2 = (f32[128,32]{0,1:T(8,128)}, f32[128,32]{0,1:T(8,128)S(1)}, u32[]{:S(2)}) copy-start(f32[128,32]{0,1:T(8,128)S(1)} %fusion.10) | copy-start | bytes 49156
Sparse Core Ops, SparseCore 0:
  16.1 58.6 all-gather.2
